TPU v7x, 128 devices: a whole 4x4x4 slice. The times are simulated.
128 devices in a mesh: dp: 8 (over y, core), feat: 16 (over z, x).
Axes of the slice: x: 4, y: 4, z: 4, core: 2. Of those that a mesh axis runs over, the one named last changes fastest.
Arguments:
- features: bfloat16 [32768, 8192], P('dp', 'feat'), may hold values from -6 to 6
- fixed_coef: float32 [8192], P('feat'), may hold values from -0.0625 to 0.0625
- member_score: float32 [32768], P('dp'), may hold values from -6 to 6
- clicks: int32 [32768], P('dp'), may hold values 0 or 1
- member_features: bfloat16 [32768, 256], P(('dp', 'feat')), may hold values from -6 to 6
- member_coef: float32 [1024, 256], P(('dp', 'feat')), may hold values from -0.375 to 0.375
- block_slot: int32 [32768], P(('dp', 'feat')), may hold values from 0 to 65535, as said below
Outputs:
- fixed_grad: float32 [8192], P('feat')
- member_coef_new: float32 [1024, 256], P(('dp', 'feat'))
- total_score: float32 [32768], P(('dp', 'feat'))
Inputs may be any that keep to these rules, and one draw needn't show every extreme that they name: All block_slot values differ. block_slot // 512 is the device (index along dp+feat) that owns the impression's member, and block_slot // 64 is the member. Every owner receives exactly 256 impressions. One device sends at most 6 of its impressions to one owner, and every device sends exactly 6 to some owner.
All inputs are finite; a program needn't handle non-finite values. Where the computation divides by a largest or mean magnitude, that divisor is 1e-20 or more. No bound on the sum of `clicks` on one device may be relied on, other than what follows from the above.
Results may differ from a plain program's by a relative error of at most 0.0093.
Values may be sent and summed in bfloat16 or wider, within the bound.
A program may use at most 64 MiB of HBM per device.

v0:
```python
import math
import jax
import jax.numpy as jnp
from jax import lax
from jax.sharding import PartitionSpec as P

BLK = 64
NEWTON = 3
ridge_weight = 1.0
high = lax.Precision.HIGHEST
inverse_sweeps = 20


def apply_inverse(system, vector):
    identity = jnp.eye(system.shape[1], dtype=system.dtype)
    bound = jnp.max(jnp.sum(jnp.abs(system), axis=2), axis=1)
    start = (2.0 / (1.0 + bound))[:, None, None] * identity[None, :, :]

    def sweep(index, approx):
        product = jnp.einsum("mbc,mcd->mbd", system, approx, precision=high)
        return 2.0 * approx - jnp.einsum("mbc,mcd->mbd", approx, product, precision=high)

    approx = lax.fori_loop(0, inverse_sweeps, sweep, start)
    return jnp.einsum("mbc,mc->mb", approx, vector, precision=high)


def newton_blocks(padded_rows, offset, label_pad, live_pad, coeffs):
    gram_matrix = jnp.einsum("mbk,mck->mbc", padded_rows, padded_rows, precision=high)
    identity = jnp.eye(padded_rows.shape[1], dtype=padded_rows.dtype)
    for iteration in range(NEWTON):
        linear = offset + jnp.einsum("mbk,mk->mb", padded_rows, coeffs, precision=high)
        probability = jax.nn.sigmoid(linear)
        gradient = (
            jnp.einsum(
                "mbk,mb->mk", padded_rows, live_pad * (probability - label_pad), precision=high
            )
            + ridge_weight * coeffs
        )
        weight_root = jnp.sqrt(live_pad * probability * (1.0 - probability))
        system = (
            ridge_weight * identity
            + weight_root[:, :, None] * gram_matrix * weight_root[:, None, :]
        )
        projected = weight_root * jnp.einsum("mbk,mk->mb", padded_rows, gradient, precision=high)
        solved = apply_inverse(system, projected)
        back_term = jnp.einsum("mbk,mb->mk", padded_rows, weight_root * solved, precision=high)
        coeffs = coeffs - (gradient - back_term) / ridge_weight
    return coeffs


def per_device(
    features, fixed_coef, member_score, clicks, member_features, member_coef, block_slot
):
    n_dp = lax.axis_size("dp")
    n_feat = lax.axis_size("feat")
    devices = n_dp * n_feat
    rows_own = member_features.shape[0]
    width = member_features.shape[1]
    slot_count = 2 * rows_own
    blocks = slot_count // BLK
    capacity = 3 * ((rows_own + devices - 1) // devices)
    row_start = lax.axis_index("feat") * rows_own
    coef_half = fixed_coef.astype(jnp.bfloat16)
    partial_score = jnp.dot(features, coef_half, preferred_element_type=jnp.float32)
    own_clicks = lax.dynamic_slice_in_dim(clicks, row_start, rows_own).astype(jnp.float32)
    fixed_score = lax.psum(partial_score, "feat")
    residual = (jax.nn.sigmoid(fixed_score + member_score) - clicks.astype(jnp.float32)).astype(
        jnp.bfloat16
    )
    own_score = lax.dynamic_slice_in_dim(fixed_score, row_start, rows_own)
    grad_part = jnp.dot(residual, features, preferred_element_type=jnp.float32)
    fixed_grad = lax.psum(grad_part, "dp") / math.sqrt(rows_own * devices)
    owner_dev = block_slot // slot_count
    local_slot = block_slot - owner_dev * slot_count
    onehot = (owner_dev[:, None] == jnp.arange(devices, dtype=jnp.int32)[None, :]).astype(jnp.int32)
    row_rank = jnp.sum(jnp.cumsum(onehot, axis=0) * onehot, axis=1) - 1
    send_place = owner_dev * capacity + row_rank
    rows_out = (
        jnp.zeros((devices * capacity, width), jnp.bfloat16).at[send_place].set(member_features)
    )
    tag_value = (local_slot * 2).astype(jnp.float32) + own_clicks
    score_buffer = jnp.zeros((devices * capacity,), jnp.float32).at[send_place].set(own_score)
    tag_buffer = jnp.full((devices * capacity,), -1.0, jnp.float32).at[send_place].set(tag_value)
    meta_out = jnp.stack([score_buffer, tag_buffer])
    rows_in = lax.all_to_all(
        rows_out.reshape(devices, capacity, width),
        ("dp", "feat"),
        split_axis=0,
        concat_axis=0,
        tiled=True,
    )
    meta_in = lax.all_to_all(
        meta_out.reshape(2, devices, capacity),
        ("dp", "feat"),
        split_axis=1,
        concat_axis=1,
        tiled=True,
    )
    rows_in = rows_in.reshape(devices * capacity, width)
    meta_in = meta_in.reshape(2, devices * capacity)
    tags_in = meta_in[1]
    valid_slot = tags_in >= 0.0
    tag_int = jnp.where(valid_slot, tags_in, 0.0).astype(jnp.int32)
    label_in = (tag_int % 2).astype(jnp.float32)
    where_local = jnp.where(valid_slot, tag_int // 2, slot_count)
    padded_rows = (
        jnp.zeros((slot_count + 1, width), jnp.float32)
        .at[where_local]
        .set(rows_in.astype(jnp.float32))[:slot_count]
        .reshape(blocks, BLK, width)
    )
    offset = (
        jnp.zeros((slot_count + 1,), jnp.float32)
        .at[where_local]
        .set(meta_in[0])[:slot_count]
        .reshape(blocks, BLK)
    )
    label_pad = (
        jnp.zeros((slot_count + 1,), jnp.float32)
        .at[where_local]
        .set(label_in)[:slot_count]
        .reshape(blocks, BLK)
    )
    live_pad = (
        jnp.zeros((slot_count + 1,), jnp.float32)
        .at[where_local]
        .set(1.0)[:slot_count]
        .reshape(blocks, BLK)
    )
    coeffs = newton_blocks(padded_rows, offset, label_pad, live_pad, member_coef)
    member_value = jnp.einsum("mbk,mk->mb", padded_rows, coeffs, precision=high).reshape(slot_count)
    back_value = jnp.where(valid_slot, member_value[jnp.minimum(where_local, slot_count - 1)], 0.0)
    returned = lax.all_to_all(
        back_value.reshape(devices, capacity),
        ("dp", "feat"),
        split_axis=0,
        concat_axis=0,
        tiled=True,
    )
    returned = returned.reshape(devices * capacity)
    total_score = own_score + returned[send_place]
    return (fixed_grad, coeffs, total_score)


def solution(mesh):
    return jax.shard_map(
        per_device,
        mesh=mesh,
        in_specs=(
            P("dp", "feat"),
            P("feat"),
            P("dp"),
            P("dp"),
            P(("dp", "feat"), None),
            P(("dp", "feat"), None),
            P(("dp", "feat")),
        ),
        out_specs=(P("feat"), P(("dp", "feat"), None), P(("dp", "feat"))),
        check_vma=False,
    )
```

profile of v0, /device:TPU:1, one launch (start us, length us, event | category | flops | bytes accessed | tf_op | source)
XLA Modules:
  0.0 235.6 jit_solution(464150204069671483)
XLA Ops:
  0.7 0.8 convert_add_fusion
  2.1 0.7 convert_element_type.65
  2.8 3.4 %fusion.54 = f32[1,4096]{1,0:T(1,128)S(1)} fusion(bf16[4096,512]{1,0:T(8,128)(2,1)} %param.13, bf16[512,1]{0,1:T(2,128)(2,1)S(1)} %reshape.293), kind=kOutput, calls=%fused_computation.124 | convolution fusion | flops 4194304 | bytes 4211712 | tf_op jit(solution)/shard_map/dot_general | solution.py:64
  6.1 62.3 %psum.14 = f32[4096]{0:T(1024)S(1)} all-reduce(f32[4096]{0:T(1024)S(1)} %bitcast.212), channel_id=1, replica_groups=mesh['dp'=8,'feat'=16] {'feat'}, use_global_device_ids=true, to_apply=%region_0.0 | all-reduce | flops 4096 | bytes 32768 | tf_op jit(solution)/shard_map/psum | solution.py:66
  68.5 1.4 scatter_custom_fusion
  70.0 1.4 scatter_custom_fusion.1
  71.6 0.8 copy.54
  72.3 18.9 %all-to-all-start = ((f32[2,128,6]{2,0,1:T(2,128)}), f32[2,128,6]{2,0,1:T(2,128)S(1)}, u32[]{:S(2)}, u32[]{:S(2)}) async-start(f32[2,128,6]{2,0,1:T(2,128)} %copy.54), calls=%async_computation | async-start | bytes 262144 | tf_op jit(solution)/shard_map/all_to_all | solution.py:92
  91.3 2.8 %fusion.55 = f32[1,512]{1,0:T(1,128)S(1)} fusion(bf16[4096,1]{0,1:T(2,128)(2,1)S(1)} %reshape.295, bf16[4096,512]{1,0:T(8,128)(2,1)} %param.13), kind=kOutput, calls=%fused_computation.125 | convolution fusion | flops 4194304 | bytes 4204544 | tf_op jit(solution)/shard_map/dot_general | solution.py:71
  94.2 12.8 %psum.15 = f32[512]{0:T(512)S(1)} all-reduce(f32[512]{0:T(512)S(1)} %bitcast.239), channel_id=1, replica_groups=mesh['dp'=8,'feat'=16] {'dp'}, use_global_device_ids=true, to_apply=%region_1.0 | all-reduce | flops 512 | bytes 4096 | tf_op jit(solution)/shard_map/psum | solution.py:72
  107.0 0.6 broadcast_multiply_fusion.3
  107.6 2.0 scatter_custom_fusion.2
  109.6 0.9 reshape.209
  110.5 9.4 %all-to-all-start.1 = ((bf16[128,6,256]{2,1,0:T(8,128)(2,1)}), bf16[128,6,256]{2,1,0:T(8,128)(2,1)S(1)}, u32[]{:S(2)}, u32[]{:S(2)}) async-start(bf16[128,6,256]{2,1,0:T(8,128)(2,1)} %reshape.209), calls=%async_computation.1 | async-start | bytes 1048576 | tf_op jit(solution)/shard_map/all_to_all | solution.py:85
  120.5 3.4 %scatter_custom_fusion.6 = f32[513]{0:T(1024)S(1)} fusion(s32[768]{0:T(1024)S(1)} %get-tuple-element.94, f32[768]{0:T(1024)S(1)} %fusion.33, f32[]{:T(128)} %constant.51.clone.1), kind=kCustom, calls=%fused_computation.98 | custom fusion | bytes 2056 | tf_op jit(solution)/shard_map/scatter | solution.py:121
  124.1 3.4 %scatter_custom_fusion.5 = f32[513]{0:T(1024)S(1)} fusion(s32[768]{0:T(1024)S(1)} %get-tuple-element.94, f32[768]{0:T(1024)S(1)} %reshape.277, f32[]{:T(128)} %constant.51.clone.1), kind=kCustom, calls=%fused_computation.100 | custom fusion | bytes 2056 | tf_op jit(solution)/shard_map/scatter | solution.py:115
  127.6 3.6 %scatter_custom_fusion.4 = f32[513]{0:T(1024)S(1)} fusion(s32[768]{0:T(1024)S(1)} %get-tuple-element.94, f32[768]{0:T(1024)S(1)} %broadcast.285, f32[]{:T(128)} %constant.51.clone.1), kind=kCustom, calls=%fused_computation.102 | custom fusion | bytes 2056 | tf_op jit(solution)/shard_map/scatter | solution.py:127
  131.2 2.8 %all-to-all-done.1 = bf16[128,6,256]{2,1,0:T(8,128)(2,1)S(1)} async-done(((bf16[128,6,256]{2,1,0:T(8,128)(2,1)}), bf16[128,6,256]{2,1,0:T(8,128)(2,1)S(1)}, u32[]{:S(2)}, u32[]{:S(2)}) %all-to-all-start.1) | async-done | bytes 393248 | tf_op jit(solution)/shard_map/all_to_all | solution.py:85
  134.1 5.6 %scatter_custom_fusion.3 = f32[513,256]{1,0:T(8,128)S(1)} fusion(s32[768]{0:T(1024)S(1)} %get-tuple-element.94, f32[768,256]{1,0:T(8,128)S(1)} %reshape.261, f32[]{:T(128)} %constant.51.clone.1), kind=kCustom, calls=%fused_computation.15 | custom fusion | bytes 525316 | tf_op jit(solution)/shard_map/scatter | solution.py:109
  139.8 0.6 fusion.27
  141.4 0.6 abs_reduce_fusion.2
  142.4 20.0 %while.30 = (s32[]{:T(128)}, f32[8,64,64]{1,2,0:T(8,128)S(1)}, f32[8,64,64]{2,1,0:T(8,128)S(1)}, s32[]{:T(128)}) while((s32[]{:T(128)}, f32[8,64,64]{1,2,0:T(8,128)S(1)}, f32[8,64,64]{2,1,0:T(8,128)S(1)}, s32[]{:T(128)}) %tuple.70), condition=%wide.region_15.16_spmd, body=%wide.region_14.15_spmd.sunk | while | flops 50397184 | bytes 1048629 | solution.py:23
  163.1 0.6 fusion.23
  165.2 20.0 %while.31 = (s32[]{:T(128)}, f32[8,64,64]{1,2,0:T(8,128)S(1)}, f32[8,64,64]{2,1,0:T(8,128)S(1)}, s32[]{:T(128)}) while((s32[]{:T(128)}, f32[8,64,64]{1,2,0:T(8,128)S(1)}, f32[8,64,64]{2,1,0:T(8,128)S(1)}, s32[]{:T(128)}) %tuple.73), condition=%wide.region_19.20_spmd, body=%wide.region_18.19_spmd.sunk | while | flops 50397184 | bytes 1048629 | solution.py:23
  188.1 20.0 %while.32 = (s32[]{:T(128)}, f32[8,64,64]{1,2,0:T(8,128)S(1)}, f32[8,64,64]{2,1,0:T(8,128)S(1)}, s32[]{:T(128)}) while((s32[]{:T(128)}, f32[8,64,64]{1,2,0:T(8,128)S(1)}, f32[8,64,64]{2,1,0:T(8,128)S(1)}, s32[]{:T(128)}) %tuple.76), condition=%wide.region_23.24_spmd, body=%wide.region_22.23_spmd.sunk | while | flops 50397184 | bytes 1048629 | solution.py:23
  209.5 5.0 %gather_fusion = f32[768]{0:T(1024)S(1)} fusion(f32[512]{0:T(512)S(1)} %reshape.214, s32[1024]{0:T(1024)S(1)} %pad_clamp_fusion.1), kind=kCustom, calls=%fused_computation | custom fusion | bytes 9216 | tf_op jit(solution)/shard_map/gather | solution.py:132
  214.7 0.6 bitcast_select_fusion.1
  215.3 7.0 %all-to-all-start.2 = ((f32[128,1,6]{2,1,0:T(1,128)}), f32[128,1,6]{2,1,0:T(1,128)S(1)}, u32[]{:S(2)}, u32[]{:S(2)}) async-start(f32[128,1,6]{2,1,0:T(1,128)} %bitcast.62), calls=%async_computation.2 | async-start | bytes 131072 | tf_op jit(solution)/shard_map/all_to_all | solution.py:133
  222.3 9.8 %all-to-all-done.2 = f32[128,1,6]{2,1,0:T(1,128)S(1)} async-done(((f32[128,1,6]{2,1,0:T(1,128)}), f32[128,1,6]{2,1,0:T(1,128)S(1)}, u32[]{:S(2)}, u32[]{:S(2)}) %all-to-all-start.2) | async-done | bytes 3104 | tf_op jit(solution)/shard_map/all_to_all | solution.py:133
  232.6 0.8 reduce.11
  233.6 1.4 gather_fusion.1
  234.9 0.6 dynamic-slice_add_fusion
  (271 shorter events, 68.3 us)
Async XLA Ops:
  0.6 90.6 %copy-start.2 = (s32[4096]{0:T(1024)S(1)}, s32[4096]{0:T(1024)}, u32[]{:S(2)}) copy-start(s32[4096]{0:T(1024)} %param.16) | copy-start | bytes 49156
  0.6 90.6 %copy-start.3 = (f32[4096]{0:T(1024)S(1)}, f32[4096]{0:T(1024)}, u32[]{:S(2)}) copy-start(f32[4096]{0:T(1024)} %param.15) | copy-start | bytes 49156
  72.3 38.2 %all-to-all-start = ((f32[2,128,6]{2,0,1:T(2,128)}), f32[2,128,6]{2,0,1:T(2,128)S(1)}, u32[]{:S(2)}, u32[]{:S(2)}) async-start(f32[2,128,6]{2,0,1:T(2,128)} %copy.54), calls=%async_computation | async-start | bytes 262144 | tf_op jit(solution)/shard_map/all_to_all | solution.py:92
  91.3 48.4 %copy-start = (f32[8,256]{1,0:T(8,128)S(1)}, f32[8,256]{1,0:T(8,128)}, u32[]{:S(2)}) copy-start(f32[8,256]{1,0:T(8,128)} %param.18) | copy-start | bytes 24580
  110.5 23.5 %all-to-all-start.1 = ((bf16[128,6,256]{2,1,0:T(8,128)(2,1)}), bf16[128,6,256]{2,1,0:T(8,128)(2,1)S(1)}, u32[]{:S(2)}, u32[]{:S(2)}) async-start(bf16[128,6,256]{2,1,0:T(8,128)(2,1)} %reshape.209), calls=%async_computation.1 | async-start | bytes 1048576 | tf_op jit(solution)/shard_map/all_to_all | solution.py:85
  208.9 26.7 %copy-start.1 = (f32[8,256]{1,0:T(8,128)}, f32[8,256]{1,0:T(8,128)S(1)}, u32[]{:S(2)}) copy-start(f32[8,256]{1,0:T(8,128)S(1)} %fusion.12) | copy-start | bytes 24580
  215.3 16.8 %all-to-all-start.2 = ((f32[128,1,6]{2,1,0:T(1,128)}), f32[128,1,6]{2,1,0:T(1,128)S(1)}, u32[]{:S(2)}, u32[]{:S(2)}) async-start(f32[128,1,6]{2,1,0:T(1,128)} %bitcast.62), calls=%async_computation.2 | async-start | bytes 131072 | tf_op jit(solution)/shard_map/all_to_all | solution.py:133
where the time goes:
time: 236 us
  blocking collectives  75.1 us (32%)
  matrix products  70.7 us (30%)
  starting transfers between devices  35.3 us (15%)
  local copies, waits for them, and re-layouts  32.6 us (14%)
  waiting for transfers between devices  12.6 us (5%)
  other arithmetic  5.86 us (2%)
    psum x1, blocking collectives, per_device(): fixed_score = lax.psum(partial_score, 'feat')  62.3 us
    dot_general x60, matrix products, sweep(): product = jnp.einsum('mbc,mcd->mbd', system, approx, precision=high)  32.8 us
    dot_general x60, matrix products, sweep(): jnp.einsum('mbc,mcd->mbd', approx, product, precision=high)  23.8 us
    all_to_all x1, starting transfers between devices, per_device(): lax.all_to_all(meta_out.reshape(2, devices, capacity), ('dp', 'feat'), sp...  18.9 us
    psum x1, blocking collectives, per_device(): fixed_grad = lax.psum(grad_part, 'dp') / math.sqrt(rows_own * devices)  12.8 us
    all_to_all x1, waiting for transfers between devices, per_device(): lax.all_to_all(back_value.reshape(devices, capacity), ('dp', 'feat'), spl...  9.8 us
    all_to_all x1, starting transfers between devices, per_device(): lax.all_to_all(rows_out.reshape(devices, capacity, width), ('dp', 'feat')...  9.4 us
    all_to_all x1, starting transfers between devices, per_device(): lax.all_to_all(back_value.reshape(devices, capacity), ('dp', 'feat'), spl...  6.99 us
  transfers between devices with their start and end apart: 3, of which 2 were waited for; matrix products, arithmetic and copies ran while one was open for 7% of the time, Pallas kernels for 0%

commit v1 on v0

--- a/solution.py
+++ b/solution.py
@@ -89,12 +89,18 @@
         concat_axis=0,
         tiled=True,
     )
-    meta_in = lax.all_to_all(
-        meta_out.reshape(2, devices, capacity),
-        ("dp", "feat"),
-        split_axis=1,
-        concat_axis=1,
-        tiled=True,
+    meta_in = jnp.concatenate(
+        lax.all_to_all(
+            jnp.stack(
+                jnp.split(
+                    meta_out.reshape(2, devices, capacity), lax.axis_size(("dp", "feat")), axis=1
+                )
+            ),
+            ("dp", "feat"),
+            0,
+            0,
+        ),
+        axis=1,
     )
     rows_in = rows_in.reshape(devices * capacity, width)
     meta_in = meta_in.reshape(2, devices * capacity)

time: 236 us -> 323 us (1.37)
  local copies, waits for them, and re-layouts: 32.6 us -> 118 us
    unnamed x9 -> x136, local copies, waits for them, and re-layouts: 0.03 us -> 72.5 us
    split x0 -> x128, local copies, waits for them, and re-layouts: none -> 12.5 us  [per_device(): jnp.split(meta_out.reshape(2, devices, capacity), lax.axis_size(('dp', 'f...]
  transfers between devices with their start and end apart: 3 -> 3, of which waited for: 2 -> 2; matrix products, arithmetic and copies ran while one was open for 7% -> 5% of each run, Pallas kernels for 0% -> 0%
where the time goes in v1:
time: 323 us
  local copies, waits for them, and re-layouts  118 us (37%)
  blocking collectives  75.1 us (23%)
  matrix products  70.3 us (22%)
  starting transfers between devices  35.2 us (11%)
  waiting for transfers between devices  12.7 us (4%)
  other arithmetic  7.83 us (2%)
    unnamed x136, local copies, waits for them, and re-layouts  72.5 us
    psum x1, blocking collectives, per_device(): fixed_score = lax.psum(partial_score, 'feat')  62.3 us
    dot_general x60, matrix products, sweep(): product = jnp.einsum('mbc,mcd->mbd', system, approx, precision=high)  32.7 us
    dot_general x60, matrix products, sweep(): jnp.einsum('mbc,mcd->mbd', approx, product, precision=high)  23.4 us
    all_to_all x1, starting transfers between devices, per_device(): lax.all_to_all(jnp.stack(jnp.split(meta_out.reshape(2, devices, capacity)...  18.9 us
    psum x1, blocking collectives, per_device(): fixed_grad = lax.psum(grad_part, 'dp') / math.sqrt(rows_own * devices)  12.8 us
    split x128, local copies, waits for them, and re-layouts, per_device(): jnp.split(meta_out.reshape(2, devices, capacity), lax.axis_size(('dp', 'f...  12.5 us
    all_to_all x1, waiting for transfers between devices, per_device(): lax.all_to_all(back_value.reshape(devices, capacity), ('dp', 'feat'), spl...  9.8 us
  transfers between devices with their start and end apart: 3, of which 2 were waited for; matrix products, arithmetic and copies ran while one was open for 5% of the time, Pallas kernels for 0%

profile of v1, /device:TPU:1, one launch (start us, length us, event | category | flops | bytes accessed | tf_op | source)
XLA Modules:
  0.0 323.0 jit_solution(7416826848060790800)
XLA Ops:
  0.6 0.8 convert_add_fusion
  2.0 0.7 convert_element_type.65
  2.7 3.4 %fusion.182 = f32[1,4096]{1,0:T(1,128)S(1)} fusion(bf16[4096,512]{1,0:T(8,128)(2,1)} %param.13, bf16[512,1]{0,1:T(2,128)(2,1)S(1)} %reshape.296), kind=kOutput, calls=%fused_computation.633 | convolution fusion | flops 4194304 | bytes 4211712 | tf_op jit(solution)/shard_map/dot_general | solution.py:64
  6.1 62.3 %psum.14 = f32[4096]{0:T(1024)S(1)} all-reduce(f32[4096]{0:T(1024)S(1)} %bitcast.477), channel_id=1, replica_groups=mesh['dp'=8,'feat'=16] {'feat'}, use_global_device_ids=true, to_apply=%region_0.0 | all-reduce | flops 4096 | bytes 32768 | tf_op jit(solution)/shard_map/psum | solution.py:66
  68.4 1.4 scatter_custom_fusion
  70.0 1.4 scatter_custom_fusion.1
  74.5 0.6 constant_dynamic-update-slice_fusion.127
  104.7 0.6 constant_dynamic-update-slice_fusion.96
  121.8 0.6 constant_dynamic-update-slice_fusion.66
  124.2 0.6 constant_dynamic-update-slice_fusion.62
  160.1 18.9 %all-to-all-start = ((f32[128,2,1,6]{3,2,1,0:T(1,128)}), f32[128,2,1,6]{3,2,1,0:T(1,128)S(1)}, u32[]{:S(2)}, u32[]{:S(2)}) async-start(f32[128,2,1,6]{3,2,1,0:T(1,128)} %bitcast.137), calls=%async_computation | async-start | bytes 262144 | tf_op jit(solution)/shard_map/all_to_all | solution.py:93
  179.1 2.8 fusion.183
  181.9 12.8 %psum.15 = f32[512]{0:T(512)S(1)} all-reduce(f32[512]{0:T(512)S(1)} %bitcast.506), channel_id=1, replica_groups=mesh['dp'=8,'feat'=16] {'dp'}, use_global_device_ids=true, to_apply=%region_1.0 | all-reduce | flops 512 | bytes 4096 | tf_op jit(solution)/shard_map/psum | solution.py:72
  195.4 2.0 scatter_custom_fusion.2
  197.3 0.9 reshape.212
  198.3 9.4 %all-to-all-start.1 = ((bf16[128,6,256]{2,1,0:T(8,128)(2,1)}), bf16[128,6,256]{2,1,0:T(8,128)(2,1)S(1)}, u32[]{:S(2)}, u32[]{:S(2)}) async-start(bf16[128,6,256]{2,1,0:T(8,128)(2,1)} %reshape.212), calls=%async_computation.1 | async-start | bytes 1048576 | tf_op jit(solution)/shard_map/all_to_all | solution.py:85
  208.5 3.4 %scatter_custom_fusion.5 = f32[513]{0:T(1024)S(1)} fusion(s32[768]{0:T(1024)S(1)} %get-tuple-element.103, f32[768]{0:T(1024)S(1)} %reshape.280, f32[]{:T(128)} %constant.51.clone.1), kind=kCustom, calls=%fused_computation.608 | custom fusion | bytes 2056 | tf_op jit(solution)/shard_map/scatter | solution.py:121
  212.0 3.4 %scatter_custom_fusion.6 = f32[513]{0:T(1024)S(1)} fusion(s32[768]{0:T(1024)S(1)} %get-tuple-element.103, f32[768]{0:T(1024)S(1)} %fusion.160, f32[]{:T(128)} %constant.51.clone.1), kind=kCustom, calls=%fused_computation.606 | custom fusion | bytes 2056 | tf_op jit(solution)/shard_map/scatter | solution.py:127
  215.4 3.4 %scatter_custom_fusion.4 = f32[513]{0:T(1024)S(1)} fusion(s32[768]{0:T(1024)S(1)} %get-tuple-element.103, f32[768]{0:T(1024)S(1)} %broadcast.285, f32[]{:T(128)} %constant.51.clone.1), kind=kCustom, calls=%fused_computation.610 | custom fusion | bytes 2056 | tf_op jit(solution)/shard_map/scatter | solution.py:133
  218.9 2.9 all-to-all-done.1
  221.9 5.6 %scatter_custom_fusion.3 = f32[513,256]{1,0:T(8,128)S(1)} fusion(s32[768]{0:T(1024)S(1)} %get-tuple-element.103, f32[768,256]{1,0:T(8,128)S(1)} %reshape.264, f32[]{:T(128)} %constant.51.clone.1), kind=kCustom, calls=%fused_computation.15 | custom fusion | bytes 525316 | tf_op jit(solution)/shard_map/scatter | solution.py:115
  229.1 0.6 abs_reduce_fusion.2
  230.1 19.9 %while.30 = (s32[]{:T(128)}, f32[8,64,64]{1,2,0:T(8,128)S(1)}, f32[8,64,64]{2,1,0:T(8,128)S(1)}, s32[]{:T(128)}) while((s32[]{:T(128)}, f32[8,64,64]{1,2,0:T(8,128)S(1)}, f32[8,64,64]{2,1,0:T(8,128)S(1)}, s32[]{:T(128)}) %tuple.186), condition=%wide.region_15.16_spmd, body=%wide.region_14.15_spmd.sunk | while | flops 50397184 | bytes 1048629 | solution.py:23
  252.9 19.9 %while.31 = (s32[]{:T(128)}, f32[8,64,64]{1,2,0:T(8,128)S(1)}, f32[8,64,64]{2,1,0:T(8,128)S(1)}, s32[]{:T(128)}) while((s32[]{:T(128)}, f32[8,64,64]{1,2,0:T(8,128)S(1)}, f32[8,64,64]{2,1,0:T(8,128)S(1)}, s32[]{:T(128)}) %tuple.189), condition=%wide.region_19.20_spmd, body=%wide.region_18.19_spmd.sunk | while | flops 50397184 | bytes 1048629 | solution.py:23
  275.6 19.9 %while.32 = (s32[]{:T(128)}, f32[8,64,64]{1,2,0:T(8,128)S(1)}, f32[8,64,64]{2,1,0:T(8,128)S(1)}, s32[]{:T(128)}) while((s32[]{:T(128)}, f32[8,64,64]{1,2,0:T(8,128)S(1)}, f32[8,64,64]{2,1,0:T(8,128)S(1)}, s32[]{:T(128)}) %tuple.192), condition=%wide.region_23.24_spmd, body=%wide.region_22.23_spmd.sunk | while | flops 50397184 | bytes 1048629 | solution.py:23
  296.9 5.0 %gather_fusion = f32[768]{0:T(1024)S(1)} fusion(f32[512]{0:T(512)S(1)} %reshape.217, s32[1024]{0:T(1024)S(1)} %pad_clamp_fusion.1), kind=kCustom, calls=%fused_computation | custom fusion | bytes 9216 | tf_op jit(solution)/shard_map/gather | solution.py:138
  302.1 0.8 copy.734
  302.8 6.9 %all-to-all-start.2 = ((f32[128,1,6]{2,1,0:T(1,128)}), f32[128,1,6]{2,1,0:T(1,128)S(1)}, u32[]{:S(2)}, u32[]{:S(2)}) async-start(f32[128,1,6]{2,1,0:T(1,128)} %copy.734), calls=%async_computation.2 | async-start | bytes 131072 | tf_op jit(solution)/shard_map/all_to_all | solution.py:139
  309.8 9.8 %all-to-all-done.2 = f32[128,1,6]{2,1,0:T(1,128)S(1)} async-done(((f32[128,1,6]{2,1,0:T(1,128)}), f32[128,1,6]{2,1,0:T(1,128)S(1)}, u32[]{:S(2)}, u32[]{:S(2)}) %all-to-all-start.2) | async-done | bytes 3104 | tf_op jit(solution)/shard_map/all_to_all | solution.py:139
  320.1 0.8 reduce.7
  321.0 1.4 gather_fusion.1
  322.4 0.6 dynamic-slice_add_fusion
  (547 shorter events, 155.7 us)
Async XLA Ops:
  2.7 176.3 %copy-start.2 = (s32[4096]{0:T(1024)S(1)}, s32[4096]{0:T(1024)}, u32[]{:S(2)}) copy-start(s32[4096]{0:T(1024)} %param.16) | copy-start | bytes 49156
  2.7 176.3 %copy-start.3 = (f32[4096]{0:T(1024)S(1)}, f32[4096]{0:T(1024)}, u32[]{:S(2)}) copy-start(f32[4096]{0:T(1024)} %param.15) | copy-start | bytes 49156
  160.1 38.2 %all-to-all-start = ((f32[128,2,1,6]{3,2,1,0:T(1,128)}), f32[128,2,1,6]{3,2,1,0:T(1,128)S(1)}, u32[]{:S(2)}, u32[]{:S(2)}) async-start(f32[128,2,1,6]{3,2,1,0:T(1,128)} %bitcast.137), calls=%async_computation | async-start | bytes 262144 | tf_op jit(solution)/shard_map/all_to_all | solution.py:93
  179.1 48.4 %copy-start = (f32[8,256]{1,0:T(8,128)S(1)}, f32[8,256]{1,0:T(8,128)}, u32[]{:S(2)}) copy-start(f32[8,256]{1,0:T(8,128)} %param.18) | copy-start | bytes 24580
  198.3 23.5 %all-to-all-start.1 = ((bf16[128,6,256]{2,1,0:T(8,128)(2,1)}), bf16[128,6,256]{2,1,0:T(8,128)(2,1)S(1)}, u32[]{:S(2)}, u32[]{:S(2)}) async-start(bf16[128,6,256]{2,1,0:T(8,128)(2,1)} %reshape.212), calls=%async_computation.1 | async-start | bytes 1048576 | tf_op jit(solution)/shard_map/all_to_all | solution.py:85
  296.2 26.8 %copy-start.1 = (f32[8,256]{1,0:T(8,128)}, f32[8,256]{1,0:T(8,128)S(1)}, u32[]{:S(2)}) copy-start(f32[8,256]{1,0:T(8,128)S(1)} %fusion.12) | copy-start | bytes 24580
  302.8 16.7 %all-to-all-start.2 = ((f32[128,1,6]{2,1,0:T(1,128)}), f32[128,1,6]{2,1,0:T(1,128)S(1)}, u32[]{:S(2)}, u32[]{:S(2)}) async-start(f32[128,1,6]{2,1,0:T(1,128)} %copy.734), calls=%async_computation.2 | async-start | bytes 131072 | tf_op jit(solution)/shard_map/all_to_all | solution.py:139
